TPU v7x, 32 devices: a whole 2x2x4 slice. The times are simulated.
32 devices in a mesh: dp: 4 (over x, core), seq: 8 (over z, y).
Axes of the slice: x: 2, y: 2, z: 4, core: 2. Of those that a mesh axis runs over, the one named last changes fastest.
Arguments:
- tile_embed: bfloat16 [4, 1024, 768], P('dp', 'seq'), may hold values from -6 to 6
- qkv_saved: bfloat16 [4, 1024, 1152], P('dp', 'seq'), may hold values from -8 to 8
- out_cotangent: bfloat16 [4, 1024, 768], P('dp', 'seq'), may hold values from -6 to 6
- qkv_weight: bfloat16 [768, 1152], replicated, may hold values from -0.21875 to 0.21875
- out_weight: bfloat16 [384, 768], replicated, may hold values from -0.3125 to 0.3125
- seg_length: int32 [8], replicated, may hold values from 128 to 1024, as said below
- dilation: int32 [8], replicated, may hold values from 1 to 4
- owner_map: int32 [4, 1024, 1], P('dp', 'seq'), may hold values from 0 to 7; in each aligned block of 128 rows (0 to 127, 128 to 255, ..., all dimensions but the last counted through in order) at most 32 rows name the same one
- tile_hidden: bfloat16 [4, 2048, 1536], P('dp', 'seq'), may hold values from -6 to 6
- tile_output: bfloat16 [4, 2048, 1536], P('dp', 'seq'), may hold values from -6 to 6
- embed_weight: bfloat16 [1536, 768], replicated, may hold values from -0.15625 to 0.15625
- proj_weight: bfloat16 [1536, 1536], replicated, may hold values from -0.15625 to 0.15625
Outputs:
- hidden_grad: bfloat16 [4, 2048, 1536], P('dp', 'seq')
- proj_weight_grad: float32 [1536, 1536], P(('dp', 'seq'))
- embed_weight_grad: float32 [1536, 768], P(('dp', 'seq'))
- qkv_weight_grad: float32 [768, 1152], P(('dp', 'seq'))
- out_weight_grad: float32 [384, 768], P(('dp', 'seq'))
Inputs may be any that keep to these rules, and one draw needn't show every extreme that they name: `seg_length`: each is 128 times a power of two; some head has 1024. `owner_map`: among the 128 positions of one device, no device index is named more than 32 times.
All inputs are finite; a program needn't handle non-finite values.
Results may differ from a plain program's by a relative error of at most 0.015.
Values may be sent and summed in bfloat16 or wider, within the bound.
A program may use at most 128 MiB of HBM per device.

v0:
```python
from functools import partial

import jax
import jax.numpy as jnp
from jax import lax
from jax.sharding import PartitionSpec as P


def head_backward(pieces, query_pos, key_pos, scaling):
    queries, keys_all, values_all, grads_out, span, stride = pieces
    allowed = (query_pos[:, None] // span == key_pos[None, :] // span) & (
        (key_pos[None, :] - query_pos[:, None]) % stride == 0
    )
    scores = (
        jnp.einsum("qd,kd->qk", queries, keys_all, preferred_element_type=jnp.float32) * scaling
    )
    scores = jnp.where(allowed, scores, -1e30)
    shifted = jnp.exp(scores - jnp.max(scores, axis=1, keepdims=True))
    probs_full = shifted / jnp.sum(shifted, axis=1, keepdims=True)
    probs_half = probs_full.astype(jnp.bfloat16)
    head_out = jnp.einsum("qk,kd->qd", probs_half, values_all, preferred_element_type=jnp.float32)
    prob_grad = jnp.einsum("qd,kd->qk", grads_out, values_all, preferred_element_type=jnp.float32)
    row_delta = jnp.sum(probs_full * prob_grad, axis=1, keepdims=True)
    score_grad = (probs_full * (prob_grad - row_delta) * scaling).astype(jnp.bfloat16)
    query_grad = jnp.einsum("qk,kd->qd", score_grad, keys_all, preferred_element_type=jnp.float32)
    key_grad = jnp.einsum("qk,qd->kd", score_grad, queries, preferred_element_type=jnp.float32)
    value_grad = jnp.einsum("qk,qd->kd", probs_half, grads_out, preferred_element_type=jnp.float32)
    return (head_out, query_grad, key_grad, value_grad)


def local(
    tile_embed,
    qkv_saved,
    out_cotangent,
    qkv_weight,
    out_weight,
    seg_length,
    dilation,
    owner_map,
    tile_hidden,
    tile_output,
    embed_weight,
    proj_weight,
):
    head_count = seg_length.shape[0]
    heads_width = out_weight.shape[0]
    head_width = heads_width // head_count
    tokens_here = qkv_saved.shape[1]
    seq_count = lax.axis_size("seq")
    length = tokens_here * seq_count
    scaling = head_width ** (-0.5)
    saved = qkv_saved[0]
    cotangent = out_cotangent[0]
    embed_rows = tile_embed[0]

    def split_heads(block):
        return block.reshape(block.shape[0], head_count, head_width).transpose(1, 0, 2)

    def merge_heads(block):
        return block.transpose(1, 0, 2).reshape(block.shape[1], heads_width)

    key_value = lax.all_gather(saved[:, heads_width:], "seq", axis=0, tiled=True)
    grads_out = jnp.einsum(
        "td,cd->tc", cotangent, out_weight, preferred_element_type=jnp.float32
    ).astype(jnp.bfloat16)
    query_pos = lax.axis_index("seq") * tokens_here + jnp.arange(tokens_here, dtype=jnp.int32)
    key_pos = jnp.arange(length, dtype=jnp.int32)
    pieces = (
        split_heads(saved[:, :heads_width]),
        split_heads(key_value[:, :heads_width]),
        split_heads(key_value[:, heads_width:]),
        split_heads(grads_out),
        seg_length,
        dilation,
    )
    head_out, query_grad, key_grad, value_grad = lax.map(
        partial(head_backward, query_pos=query_pos, key_pos=key_pos, scaling=scaling), pieces
    )
    attention = merge_heads(head_out).astype(jnp.bfloat16)
    partials = jnp.concatenate([merge_heads(key_grad), merge_heads(value_grad)], axis=1)
    summed = lax.psum_scatter(
        partials.astype(jnp.bfloat16), "seq", scatter_dimension=0, tiled=True
    ).astype(jnp.float32)
    qkv_grad = jnp.concatenate([merge_heads(query_grad), summed], axis=1).astype(jnp.bfloat16)
    embed_grad = (
        cotangent.astype(jnp.float32)
        + jnp.einsum("tc,dc->td", qkv_grad, qkv_weight, preferred_element_type=jnp.float32)
    ).astype(jnp.bfloat16)
    columns = embed_rows
    qkv_sum = lax.psum_scatter(
        jnp.einsum("tc,tk->ck", columns, qkv_grad, preferred_element_type=jnp.float32),
        ("dp", "seq"),
        scatter_dimension=0,
        tiled=True,
    )
    columns = attention
    out_sum = lax.psum_scatter(
        jnp.einsum("tc,tk->ck", columns, cotangent, preferred_element_type=jnp.float32),
        ("dp", "seq"),
        scatter_dimension=0,
        tiled=True,
    )
    destination = owner_map[0, :, 0]
    capacity = tile_hidden.shape[1] // seq_count
    onehot = (destination[:, None] == jnp.arange(seq_count, dtype=jnp.int32)[None, :]).astype(
        jnp.int32
    )
    before = jnp.cumsum(onehot, axis=0) - onehot
    slot_index = destination * capacity + jnp.sum(before * onehot, axis=1)
    selector = (
        jnp.arange(seq_count * capacity, dtype=jnp.int32)[:, None] == slot_index[None, :]
    ).astype(jnp.bfloat16)
    outgoing = jnp.dot(selector, embed_grad, preferred_element_type=jnp.float32).astype(
        jnp.bfloat16
    )
    outgoing = outgoing.reshape(seq_count, capacity, embed_grad.shape[1])
    incoming = lax.all_to_all(outgoing, "seq", split_axis=0, concat_axis=0, tiled=True).reshape(
        seq_count * capacity, embed_grad.shape[1]
    )
    hidden_rows = tile_hidden[0]
    output_rows = tile_output[0]
    tile_grad = jnp.einsum("sd,ed->se", incoming, embed_weight, preferred_element_type=jnp.float32)
    grad_high = tile_grad.astype(jnp.bfloat16)
    hidden_grad = jnp.einsum(
        "se,fe->sf", grad_high, proj_weight, preferred_element_type=jnp.float32
    ).astype(jnp.bfloat16)[None]
    columns = output_rows
    embed_sum = lax.psum_scatter(
        jnp.einsum("sc,sd->cd", columns, incoming, preferred_element_type=jnp.float32),
        ("dp", "seq"),
        scatter_dimension=0,
        tiled=True,
    )
    columns = hidden_rows
    factor = lax.psum_scatter(
        jnp.einsum("sc,sd->cd", columns, incoming, preferred_element_type=jnp.float32),
        ("dp", "seq"),
        scatter_dimension=0,
        tiled=True,
    )
    proj_sum = jnp.dot(factor, embed_weight.astype(jnp.float32).T, precision=lax.Precision.HIGHEST)
    return (hidden_grad, proj_sum, embed_sum, qkv_sum, out_sum)


def solution(mesh):
    return jax.shard_map(
        local,
        mesh=mesh,
        in_specs=(
            P("dp", "seq", None),
            P("dp", "seq", None),
            P("dp", "seq", None),
            P(),
            P(),
            P(),
            P(),
            P("dp", "seq", None),
            P("dp", "seq", None),
            P("dp", "seq", None),
            P(),
            P(),
        ),
        out_specs=(
            P("dp", "seq", None),
            P(("dp", "seq"), None),
            P(("dp", "seq"), None),
            P(("dp", "seq"), None),
            P(("dp", "seq"), None),
        ),
        check_vma=False,
    )
```

profile of v0, /device:TPU:0, one launch (start us, length us, event | category | flops | bytes accessed | tf_op | source)
XLA Modules:
  0.0 657.8 jit_solution(4617491847671271534)
XLA Ops:
  12.2 45.6 %all-gather.2.cloned.1.call-done = bf16[1024,768]{0,1:T(8,128)(2,1)} async-done(((bf16[128,768]{0,1:T(8,128)(2,1)}), bf16[1024,768]{0,1:T(8,128)(2,1)}) %all-gather.2.cloned.1.call-update) | async-done | bytes 1572880 | tf_op jit(solution)/shard_map/all_gather | solution.py:62
  57.8 2.4 fusion.69
  60.2 142.0 %while.22 = (s32[]{:T(128)}, bf16[8,128,48]{1,2,0:T(8,128)(2,1)}, bf16[8,128,48]{1,2,0:T(8,128)(2,1)S(1)}, bf16[8,1024,48]{1,2,0:T(8,128)(2,1)}, bf16[8,1024,48]...) while((s32[]{:T(128)}, bf16[8,128,48]{1,2,0:T(8,128)(2,1)}, ...), condition=%wide.region_6.7_spmd.clone.clone.clone, body=%wide.region_2.6_spmd.clone.clone.clone.sunk | while | flops 79700864 | bytes 5890781 | solution.py:76
  64.9 6.1 fusion.107
  82.6 6.1 fusion.107
  100.4 6.1 fusion.107
  118.1 6.1 fusion.107
  135.8 6.1 fusion.107
  153.6 6.1 fusion.107
  171.3 6.1 fusion.107
  189.1 6.1 fusion.107
  202.1 2.7 pad_maximum_fusion
  204.8 2.6 copy.36
  207.5 64.0 %reduce-scatter.13.cloned.1.call-done = bf16[128,768]{1,0:T(8,128)(2,1)} async-done(((bf16[1024,768]{1,0:T(8,128)(2,1)}), bf16[128,768]{1,0:T(8,128)(2,1)}) %reduce-scatter.13.cloned.1.call-update) | async-done | bytes 196624
  272.6 2.4 convolution_bitcast_fusion.4
  276.1 2.4 convolution_convert_fusion.2
  278.5 20.1 %all_to_all.5 = bf16[8,32,768]{2,1,0:T(8,128)(2,1)S(1)} all-to-all(bf16[8,32,768]{2,1,0:T(8,128)(2,1)S(1)} %bitcast.168), channel_id=1, replica_groups=mesh['dp'=4,'seq'=8] {'seq'}, dimensions={0} | all-to-all | bytes 786432 | tf_op jit(solution)/shard_map/all_to_all | solution.py:117
  298.6 4.1 convolution_bitcast_fusion.6
  302.7 6.1 copy.38
  309.1 4.2 convolution_bitcast_fusion.5
  313.3 6.1 copy.40
  319.4 2.2 fusion.59
  321.6 79.1 %fusion.8 = f32[16,768]{1,0:T(8,128)S(1)} fusion(f32[384,768]{1,0:T(8,128)} %fusion.59), kind=kCustom, calls=%all-reduce-scatter | all-reduce-scatter fusion | flops 393217 | bytes 1228800
  400.7 2.7 collective-permute-start
  407.3 8.7 %collective-permute-start.3 = (f32[16,768]{1,0:T(8,128)S(1)}, f32[16,768]{1,0:T(8,128)S(1)}, u32[]{:S(2)}, u32[]{:S(2)}) collective-permute-start(f32[16,768]{1,0:T(8,128)S(1)} %fusion.8), channel_id=1, source_target_pairs={{0,4},{1,5},{2,6},{3,7},{4,8},{5,9},{6,10},{7,11},{8,12},{9,13},{1... | collective-permute-start | bytes 147464
  417.7 4.9 collective-permute-start.5
  422.6 2.5 collective-permute-start.6
  426.3 2.5 concatenate.10
  429.5 5.3 fusion.53
  437.1 101.8 %reduce-scatter.15.cloned.1.call-done = f32[48,768]{1,0:T(8,128)} async-done(((f32[1536,768]{1,0:T(8,128)}), f32[48,768]{1,0:T(8,128)}) %reduce-scatter.15.cloned.1.call-update) | async-done | bytes 147472
  538.8 3.8 fusion.70
  542.6 108.6 %reduce-scatter.17.cloned.1.call-done = f32[48,768]{1,0:T(8,128)} async-done(((f32[1536,768]{1,0:T(8,128)}), f32[48,768]{1,0:T(8,128)}) %reduce-scatter.17.cloned.1.call-update) | async-done | bytes 147472
  (151 shorter events, 94.2 us)
Async XLA Ops:
  7.2 422.3 %copy-start = (bf16[1536,768]{1,0:T(8,128)(2,1)S(1)}, bf16[1536,768]{1,0:T(8,128)(2,1)}, u32[]{:S(2)}) copy-start(bf16[1536,768]{1,0:T(8,128)(2,1)} %param.24) | copy-start | bytes 7077892
  7.2 50.6 %all-gather.2.cloned.1.call-start = ((), (), s32[]{:S(2)}) async-start(), calls=%async_computation.4 | async-start | bytes 1769472 | tf_op jit(solution)/shard_map/all_gather | solution.py:62
  9.2 50.9 %copy-start.5 = (s32[8]{0:T(128)S(1)}, s32[8]{0:T(128)}, u32[]{:S(2)}) copy-start(s32[8]{0:T(128)} %param.19) | copy-start | bytes 100
  9.2 50.9 %copy-start.6 = (s32[8]{0:T(128)S(1)}, s32[8]{0:T(128)}, u32[]{:S(2)}) copy-start(s32[8]{0:T(128)} %param.20) | copy-start | bytes 100
  9.3 262.2 %reduce-scatter.13.cloned.1.call-start = ((), (), s32[]{:S(2)}) async-start(), calls=%async_computation.5 | async-start | bytes 1769472
  204.8 67.8 %copy-start.2 = (bf16[1,128,768]{2,1,0:T(8,128)(2,1)S(1)}, bf16[1,128,768]{2,1,0:T(8,128)(2,1)}, u32[]{:S(2)}) copy-start(bf16[1,128,768]{2,1,0:T(8,128)(2,1)} %param.14) | copy-start | bytes 589828
  207.5 227.3 %all-reduce.5.cloned.1.call-start = ((), (), s32[]{:S(2)}) async-start(), calls=%async_computation.8 | async-start | bytes 7077888
  275.0 0.7 copy-start.4
  275.0 1.1 copy-start.1
  275.0 263.9 %reduce-scatter.15.cloned.1.call-start = ((), (), s32[]{:S(2)}) async-start(), calls=%async_computation.6 | async-start | bytes 4866048
  308.8 342.4 %reduce-scatter.17.cloned.1.call-start = ((), (), s32[]{:S(2)}) async-start(), calls=%async_computation.7 | async-start | bytes 4866048
  400.7 17.0 %collective-permute-start = (f32[16,768]{1,0:T(8,128)S(1)}, f32[16,768]{1,0:T(8,128)S(1)}, u32[]{:S(2)}, u32[]{:S(2)}) collective-permute-start(f32[16,768]{1,0:T(8,128)S(1)} %fusion.8), channel_id=1, source_target_pairs={{0,1},{1,2},{2,3},{3,4},{4,5},{5,6},{6,7},{7,8},{8,9},{9,10},{10,1... | collective-permute-start | bytes 147464
  403.4 19.2 %collective-permute-start.1 = (f32[16,768]{1,0:T(8,128)S(1)}, f32[16,768]{1,0:T(8,128)S(1)}, u32[]{:S(2)}, u32[]{:S(2)}) collective-permute-start(f32[16,768]{1,0:T(8,128)S(1)} %fusion.8), channel_id=1, source_target_pairs={{0,2},{1,3},{2,4},{3,5},{4,6},{5,7},{6,8},{7,9},{8,10},{9,11},{10,... | collective-permute-start | bytes 147464
  404.7 11.4 %collective-permute-start.7 = (f32[12,768]{1,0:T(8,128)S(1)}, f32[12,768]{1,0:T(8,128)S(1)}, u32[]{:S(2)}, u32[]{:S(2)}) collective-permute-start(f32[12,768]{1,0:T(8,128)S(1)} %slice.20), channel_id=1, source_target_pairs={{0,8},{1,9},{2,10},{3,11},{4,12},{5,13},{6,14},{7,15},{8,16},{9,17... | collective-permute-start | bytes 110600
  406.0 19.2 %collective-permute-start.2 = (f32[16,768]{1,0:T(8,128)S(1)}, f32[16,768]{1,0:T(8,128)S(1)}, u32[]{:S(2)}, u32[]{:S(2)}) collective-permute-start(f32[16,768]{1,0:T(8,128)S(1)} %fusion.8), channel_id=1, source_target_pairs={{0,3},{1,4},{2,5},{3,6},{4,7},{5,8},{6,9},{7,10},{8,11},{9,12},{10... | collective-permute-start | bytes 147464
  407.3 17.9 %collective-permute-start.3 = (f32[16,768]{1,0:T(8,128)S(1)}, f32[16,768]{1,0:T(8,128)S(1)}, u32[]{:S(2)}, u32[]{:S(2)}) collective-permute-start(f32[16,768]{1,0:T(8,128)S(1)} %fusion.8), channel_id=1, source_target_pairs={{0,4},{1,5},{2,6},{3,7},{4,8},{5,9},{6,10},{7,11},{8,12},{9,13},{1... | collective-permute-start | bytes 147464
  416.1 9.1 %collective-permute-start.4 = (f32[16,768]{1,0:T(8,128)S(1)}, f32[16,768]{1,0:T(8,128)S(1)}, u32[]{:S(2)}, u32[]{:S(2)}) collective-permute-start(f32[16,768]{1,0:T(8,128)S(1)} %fusion.8), channel_id=1, source_target_pairs={{0,5},{1,6},{2,7},{3,8},{4,9},{5,10},{6,11},{7,12},{8,13},{9,14},{... | collective-permute-start | bytes 147464
  417.7 7.5 %collective-permute-start.5 = (f32[16,768]{1,0:T(8,128)S(1)}, f32[16,768]{1,0:T(8,128)S(1)}, u32[]{:S(2)}, u32[]{:S(2)}) collective-permute-start(f32[16,768]{1,0:T(8,128)S(1)} %fusion.8), channel_id=1, source_target_pairs={{0,6},{1,7},{2,8},{3,9},{4,10},{5,11},{6,12},{7,13},{8,14},{9,15},... | collective-permute-start | bytes 147464
  422.6 3.7 collective-permute-start.6
  425.2 0.6 copy-start.3
Sparse Core Ops, SparseCore 0:
  10.6 47.1 all-gather.1
  207.6 63.8 reduce-scatter.12
  277.1 151.0 all-reduce.4
  433.6 105.2 reduce-scatter.14
  544.7 106.4 reduce-scatter.16
where the time goes:
time: 661 us; the launch traced here: 658 us
  waiting for transfers between devices  321 us (49%)
  matrix products  126 us (19%)
  blocking collectives  99.2 us (15%)
  local copies, waits for them, and re-layouts  37.8 us (6%)
  starting transfers between devices  24.8 us (4%)
  other arithmetic  19.4 us (3%)
  loops' own time  15.8 us (2%)
  between operations  14 us (2%)
    unnamed x17, waiting for transfers between devices  275 us
    unnamed x1, blocking collectives  79.1 us
    dot_general x8, matrix products, head_backward(): jnp.einsum('qd,kd->qk', queries, keys_all, preferred_element_type=jnp.flo...  49.1 us
    all_gather x1, waiting for transfers between devices, local(): lax.all_gather(saved[:, heads_width:], 'seq', axis=0, tiled=True)  45.6 us
    unnamed x12, starting transfers between devices  24.7 us
    unnamed x24, local copies, waits for them, and re-layouts  24 us
    all_to_all x1, blocking collectives, local(): lax.all_to_all(outgoing, 'seq', split_axis=0, concat_axis=0, tiled=True)  20.1 us
    another operation x1, loops' own time, local(): lax.map(partial(head_backward, query_pos=query_pos, key_pos=key_pos, scal...  15.8 us
  transfers between devices with their start and end apart: 13, of which 5 were waited for; matrix products, arithmetic and copies ran while one was open for 19% of the time, Pallas kernels for 0%

commit v1 on v0

--- a/solution.py
+++ b/solution.py
@@ -3,7 +3,14 @@
 import jax
 import jax.numpy as jnp
 from jax import lax
+from jax.experimental import pallas as pl
+from jax.experimental.pallas import tpu as pltpu
 from jax.sharding import PartitionSpec as P
+
+
+MESH = pl.DeviceIdType.MESH
+BF16 = jnp.bfloat16
+F32 = jnp.float32
 
 
 def head_backward(pieces, query_pos, key_pos, scaling):
@@ -142,9 +149,409 @@
     return (hidden_grad, proj_sum, embed_sum, qkv_sum, out_sum)
 
 
+def greet(peers):
+    barrier = pltpu.get_barrier_semaphore()
+    for peer in peers:
+        pl.semaphore_signal(barrier, inc=1, device_id=peer, device_id_type=MESH)
+    pl.semaphore_wait(barrier, len(peers))
+
+
+def swap_blocks(source, target, send_sems, recv_sems, count):
+    me = lax.axis_index("seq")
+    copies = []
+    for step in range(1, count):
+        peer = lax.rem(me + step, count)
+        copy = pltpu.make_async_remote_copy(
+            src_ref=source.at[peer],
+            dst_ref=target.at[me],
+            send_sem=send_sems.at[step - 1],
+            recv_sem=recv_sems.at[step - 1],
+            device_id=(lax.axis_index("dp"), peer),
+            device_id_type=MESH,
+        )
+        copy.start()
+        copies.append(copy)
+    return copies
+
+
+def seq_peers(count):
+    me = lax.axis_index("seq")
+    return [(lax.axis_index("dp"), lax.rem(me + step, count)) for step in range(1, count)]
+
+
+def exchange_kernel(count, source, target, send_sems, recv_sems, local_sem):
+    me = lax.axis_index("seq")
+    greet(seq_peers(count))
+    own = pltpu.make_async_copy(source.at[me], target.at[me], local_sem)
+    own.start()
+    copies = swap_blocks(source, target, send_sems, recv_sems, count)
+    own.wait()
+    for copy in copies:
+        copy.wait()
+
+
+def exchange(blocks):
+    count = blocks.shape[0]
+    return pl.pallas_call(
+        partial(exchange_kernel, count),
+        out_shape=jax.ShapeDtypeStruct(blocks.shape, blocks.dtype),
+        in_specs=[pl.BlockSpec(memory_space=pltpu.VMEM)],
+        out_specs=pl.BlockSpec(memory_space=pltpu.VMEM),
+        scratch_shapes=[
+            pltpu.SemaphoreType.DMA((count - 1,)),
+            pltpu.SemaphoreType.DMA((count - 1,)),
+            pltpu.SemaphoreType.DMA,
+        ],
+        compiler_params=pltpu.CompilerParams(collective_id=1, has_side_effects=True),
+        name="tile_exchange",
+    )(blocks)
+
+
+def attention_kernel(
+    count,
+    width,
+    scaling,
+    source,
+    id_column,
+    id_row,
+    result,
+    arrived,
+    outgoing,
+    ids,
+    keys_t,
+    values_t,
+    keys_n,
+    values_n,
+    key_total,
+    value_total,
+    send_sems,
+    recv_sems,
+    back_send,
+    back_recv,
+    local_sems,
+):
+    me = lax.axis_index("seq")
+    tokens = source.shape[2]
+    length = count * tokens
+    greet(seq_peers(count))
+    own = pltpu.make_async_copy(source.at[me], arrived.at[me], local_sems.at[0])
+    own.start()
+    copies = swap_blocks(source, arrived, send_sems, recv_sems, count)
+    ids[...] = jnp.broadcast_to(id_column[...], (length, tokens))
+    key_total[...] = jnp.zeros_like(key_total)
+    value_total[...] = jnp.zeros_like(value_total)
+    own.wait()
+    for copy in copies:
+        copy.wait()
+    for block in range(count):
+        lanes = slice(block * tokens, (block + 1) * tokens)
+        key_block = arrived[block, width : 2 * width, :]
+        value_block = arrived[block, 2 * width : 3 * width, :]
+        keys_t[:, lanes] = key_block
+        values_t[:, lanes] = value_block
+        keys_n[lanes, :] = key_block.astype(F32).T.astype(BF16)
+        values_n[lanes, :] = value_block.astype(F32).T.astype(BF16)
+
+    def one_block(block, carry):
+        queries = arrived[block, 0:width, :]
+        grads = arrived[block, 3 * width : 4 * width, :]
+        scores = jnp.dot(keys_n[...], queries, preferred_element_type=F32) * scaling
+        scores = jnp.where(ids[...] == id_row[block], scores, -1e30)
+        shifted = jnp.exp(scores - jnp.max(scores, axis=0, keepdims=True))
+        probs = shifted * (1.0 / jnp.sum(shifted, axis=0, keepdims=True))
+        probs_half = probs.astype(BF16)
+        head_out = jnp.dot(values_t[...], probs_half, preferred_element_type=F32)
+        prob_grad = jnp.dot(values_n[...], grads, preferred_element_type=F32)
+        row_delta = jnp.sum(probs * prob_grad, axis=0, keepdims=True)
+        score_grad = (probs * (prob_grad - row_delta) * scaling).astype(BF16)
+        query_grad = jnp.dot(keys_t[...], score_grad, preferred_element_type=F32)
+        last = (((1,), (1,)), ((), ()))
+        key_total[...] += lax.dot_general(queries, score_grad, last, preferred_element_type=F32)
+        value_total[...] += lax.dot_general(grads, probs_half, last, preferred_element_type=F32)
+        outgoing[block, 0:width, :] = head_out.astype(BF16)
+        outgoing[block, width : 2 * width, :] = query_grad.astype(BF16)
+        return carry
+
+    lax.fori_loop(0, count, one_block, 0)
+    for block in range(count):
+        lanes = slice(block * tokens, (block + 1) * tokens)
+        outgoing[block, 2 * width : 3 * width, :] = key_total[:, lanes].astype(BF16)
+        outgoing[block, 3 * width : 4 * width, :] = value_total[:, lanes].astype(BF16)
+    own = pltpu.make_async_copy(outgoing.at[me], result.at[me], local_sems.at[1])
+    own.start()
+    copies = swap_blocks(outgoing, result, back_send, back_recv, count)
+    own.wait()
+    for copy in copies:
+        copy.wait()
+
+
+def attention_by_head(blocks, ids, width, scaling):
+    count, _, tokens = blocks.shape
+    length = count * tokens
+    vmem = pl.BlockSpec(memory_space=pltpu.VMEM)
+    sems = pltpu.SemaphoreType.DMA((count - 1,))
+    return pl.pallas_call(
+        partial(attention_kernel, count, width, scaling),
+        out_shape=jax.ShapeDtypeStruct(blocks.shape, BF16),
+        in_specs=[vmem] * 3,
+        out_specs=vmem,
+        scratch_shapes=[
+            pltpu.VMEM(blocks.shape, BF16),
+            pltpu.VMEM(blocks.shape, BF16),
+            pltpu.VMEM((length, tokens), jnp.int32),
+            pltpu.VMEM((width, length), BF16),
+            pltpu.VMEM((width, length), BF16),
+            pltpu.VMEM((length, width), BF16),
+            pltpu.VMEM((length, width), BF16),
+            pltpu.VMEM((width, length), F32),
+            pltpu.VMEM((width, length), F32),
+            sems,
+            sems,
+            sems,
+            sems,
+            pltpu.SemaphoreType.DMA((2,)),
+        ],
+        compiler_params=pltpu.CompilerParams(collective_id=0, has_side_effects=True),
+        name="head_attention",
+    )(blocks, ids[:, None], ids.reshape(count, 1, tokens))
+
+
+def reduce_kernel(bit_counts, orders, *refs):
+    streams = len(orders)
+    bits = sum(bit_counts)
+    dp_bits, seq_bits = bit_counts
+    sources, results = refs[:streams], refs[streams : 2 * streams]
+    held = refs[2 * streams : 3 * streams]
+    landing = refs[3 * streams : 3 * streams + streams * bits]
+    send_sems, recv_sems = refs[3 * streams + streams * bits :]
+    dp, seq = lax.axis_index("dp"), lax.axis_index("seq")
+    mine = [(dp // 2 ** (dp_bits - 1 - b)) % 2 for b in range(dp_bits)]
+    mine += [(seq // 2 ** (seq_bits - 1 - b)) % 2 for b in range(seq_bits)]
+
+    def partner(bit):
+        if bit < dp_bits:
+            return (dp + (1 - 2 * mine[bit]) * 2 ** (dp_bits - 1 - bit), seq)
+        return (dp, seq + (1 - 2 * mine[bit]) * 2 ** (bits - 1 - bit))
+
+    greet([partner(bit) for bit in range(bits)])
+    copies = {}
+
+    def start(stream, stage):
+        order = orders[stream]
+        done, now = order[:stage], order[stage]
+        buffer = sources[stream] if stage == 0 else held[stream]
+        index = []
+        for bit in range(bits):
+            if stage > 0 and bit == order[0]:
+                continue
+            if bit in done:
+                index.append(mine[bit])
+            elif bit == now:
+                index.append(1 - mine[bit])
+            else:
+                index.append(slice(None))
+        copy = pltpu.make_async_remote_copy(
+            src_ref=buffer.at[tuple(index)],
+            dst_ref=landing[stream * bits + stage],
+            send_sem=send_sems.at[stream * bits + stage],
+            recv_sem=recv_sems.at[stream * bits + stage],
+            device_id=partner(now),
+            device_id_type=MESH,
+        )
+        copy.start()
+        copies[stream, stage] = copy
+
+    def add(stream, stage):
+        order = orders[stream]
+        open_bits = [bit for bit in range(bits) if bit not in order[: stage + 1]]
+        target = landing[stream * bits + stage]
+
+        def place(step):
+            chosen = {}
+            for rank, bit in enumerate(open_bits):
+                chosen[bit] = (step // 2 ** (len(open_bits) - 1 - rank)) % 2
+            full = [chosen.get(bit, mine[bit]) for bit in range(bits)]
+            small = [full[bit] for bit in range(bits) if bit != order[0]]
+            return tuple(full), tuple(small), tuple(chosen[bit] for bit in open_bits)
+
+        def one(step, carry):
+            full, small, inner = place(step)
+            kept = sources[stream][full] if stage == 0 else held[stream][small]
+            total = kept.astype(F32) + target[inner].astype(F32)
+            if stage == bits - 1:
+                results[stream][...] = total
+            else:
+                held[stream][small] = total.astype(BF16)
+            return carry
+
+        if open_bits:
+            lax.fori_loop(0, 2 ** len(open_bits), one, 0)
+        else:
+            one(0, 0)
+
+    for stream in range(streams):
+        start(stream, 0)
+    for stage in range(bits):
+        for stream in range(streams):
+            copies[stream, stage].wait_recv()
+            add(stream, stage)
+            if stage + 1 < bits:
+                start(stream, stage + 1)
+    for copy in copies.values():
+        copy.wait_send()
+
+
+def reduce_blocks(arrays, bit_counts, orders):
+    bits = sum(bit_counts)
+    shaped = [array.reshape((2,) * bits + array.shape[1:]) for array in arrays]
+    streams = len(arrays)
+    vmem = pl.BlockSpec(memory_space=pltpu.VMEM)
+    held = [pltpu.VMEM((2,) * (bits - 1) + array.shape[1:], BF16) for array in arrays]
+    landing = [
+        pltpu.VMEM((2,) * (bits - 1 - stage) + array.shape[1:], BF16)
+        for array in arrays
+        for stage in range(bits)
+    ]
+    return pl.pallas_call(
+        partial(reduce_kernel, bit_counts, orders),
+        out_shape=[jax.ShapeDtypeStruct(array.shape[1:], F32) for array in arrays],
+        in_specs=[vmem] * streams,
+        out_specs=[vmem] * streams,
+        scratch_shapes=held
+        + landing
+        + [pltpu.SemaphoreType.DMA((streams * bits,)), pltpu.SemaphoreType.DMA((streams * bits,))],
+        compiler_params=pltpu.CompilerParams(collective_id=2, has_side_effects=True),
+        name="reduce_blocks",
+    )(*shaped)
+
+
+def split_product(left, right):
+    high = left.astype(BF16)
+    low = (left - high.astype(F32)).astype(BF16)
+    both = jnp.concatenate([high, low], axis=0)
+    product = jnp.einsum("sd,ed->se", both, right, preferred_element_type=F32)
+    return product[: left.shape[0]] + product[left.shape[0] :]
+
+
+def route(owners, embed_grad, seq_count, capacity):
+    onehot = (owners[:, None] == jnp.arange(seq_count, dtype=jnp.int32)[None, :]).astype(BF16)
+    tokens = owners.shape[0]
+    earlier = (jnp.arange(tokens)[:, None] > jnp.arange(tokens)[None, :]).astype(BF16)
+    before = jnp.dot(earlier, onehot, preferred_element_type=F32)
+    rank = jnp.sum(before * onehot.astype(F32), axis=1).astype(jnp.int32)
+    slot_index = owners * capacity + rank
+    selector = (
+        jnp.arange(seq_count * capacity, dtype=jnp.int32)[:, None] == slot_index[None, :]
+    ).astype(BF16)
+    outgoing = jnp.dot(selector, embed_grad, preferred_element_type=F32).astype(BF16)
+    return outgoing.reshape(seq_count, capacity, embed_grad.shape[1])
+
+
+def local_by_head(
+    tile_embed,
+    qkv_saved,
+    out_cotangent,
+    qkv_weight,
+    out_weight,
+    seg_length,
+    dilation,
+    owner_map,
+    tile_hidden,
+    tile_output,
+    embed_weight,
+    proj_weight,
+):
+    head_count = seg_length.shape[0]
+    heads_width = out_weight.shape[0]
+    width = heads_width // head_count
+    tokens = qkv_saved.shape[1]
+    seq_count = lax.axis_size("seq")
+    dp_count = lax.axis_size("dp")
+    devices = seq_count * dp_count
+    bit_counts = (dp_count.bit_length() - 1, seq_count.bit_length() - 1)
+    length = tokens * seq_count
+    cotangent, embed_rows = out_cotangent[0], tile_embed[0]
+    grads_out = jnp.einsum("cd,td->ct", out_weight, cotangent, preferred_element_type=F32)
+    blocks = jnp.concatenate([qkv_saved[0].T, grads_out.astype(BF16)], axis=0)
+    blocks = blocks.reshape(4, head_count, width, tokens).transpose(1, 0, 2, 3)
+    blocks = blocks.reshape(head_count, 4 * width, tokens)
+    head = lax.axis_index("seq")
+    span = lax.dynamic_index_in_dim(seg_length, head, keepdims=False)
+    stride = lax.dynamic_index_in_dim(dilation, head, keepdims=False)
+    pos = jnp.arange(length, dtype=jnp.int32)
+    ids = pos // span * stride + pos % stride
+    returned = attention_by_head(blocks, ids, width, width ** (-0.5))
+    parts = returned.reshape(head_count, 4, width, tokens).transpose(1, 0, 2, 3)
+    attention = parts[0].reshape(heads_width, tokens)
+    qkv_grad = parts[1:].reshape(3 * heads_width, tokens)
+    embed_grad = (
+        cotangent.astype(F32)
+        + jnp.einsum("ct,dc->td", qkv_grad, qkv_weight, preferred_element_type=F32)
+    ).astype(BF16)
+    capacity = tile_hidden.shape[1] // seq_count
+    incoming = exchange(route(owner_map[0, :, 0], embed_grad, seq_count, capacity))
+    incoming = incoming.reshape(seq_count * capacity, embed_grad.shape[1])
+
+    qkv_term = jnp.einsum("tc,kt->ck", embed_rows, qkv_grad, preferred_element_type=F32)
+    out_term = jnp.einsum("ct,tk->ck", attention, cotangent, preferred_element_type=F32)
+    qkv_rows = qkv_weight.shape[0] // devices
+    out_rows = heads_width // devices
+    qkv_cols = qkv_weight.shape[1]
+    packed = out_rows * out_weight.shape[1] // qkv_cols
+    slide_terms = jnp.concatenate(
+        [
+            qkv_term.astype(BF16).reshape(devices, qkv_rows, qkv_cols),
+            out_term.astype(BF16).reshape(devices, packed, qkv_cols),
+        ],
+        axis=1,
+    )
+    embed_term = jnp.einsum("sc,sd->cd", tile_output[0], incoming, preferred_element_type=F32)
+    factor_term = jnp.einsum("sc,sd->cd", tile_hidden[0], incoming, preferred_element_type=F32)
+    tile_rows = embed_weight.shape[0] // devices
+    tile_shape = (devices, tile_rows, embed_weight.shape[1])
+    tile_grad = jnp.einsum("sd,ed->se", incoming, embed_weight, preferred_element_type=F32)
+    hidden_grad = jnp.einsum(
+        "se,fe->sf", tile_grad.astype(BF16), proj_weight, preferred_element_type=F32
+    ).astype(BF16)[None]
+    dp_bits, bits = bit_counts[0], sum(bit_counts)
+    core = dp_bits - 1
+    high = list(range(dp_bits - 1))
+    low = list(range(dp_bits, bits))
+    orders = (
+        [core] + high + low[::-1],
+        [core] + low[::-1][:1] + high + low[::-1][1:],
+        [core] + low[1:2] + high + low[2:] + low[:1],
+    )
+    slide_sum, embed_sum, factor = reduce_blocks(
+        [
+            slide_terms,
+            embed_term.astype(BF16).reshape(tile_shape),
+            factor_term.astype(BF16).reshape(tile_shape),
+        ],
+        bit_counts,
+        orders,
+    )
+    proj_sum = split_product(factor, embed_weight)
+    qkv_sum = slide_sum[:qkv_rows]
+    out_sum = slide_sum[qkv_rows:].reshape(out_rows, out_weight.shape[1])
+    return (hidden_grad, proj_sum, embed_sum, qkv_sum, out_sum)
+
+
+def pick(*args):
+    head_count = args[5].shape[0]
+    heads_width = args[4].shape[0]
+    seq_count, dp_count = lax.axis_size("seq"), lax.axis_size("dp")
+    devices = seq_count * dp_count
+    fits = head_count == seq_count and (heads_width // head_count) % 16 == 0
+    fits = fits and dp_count > 1 and devices & (devices - 1) == 0
+    fits = fits and args[10].shape[0] % (16 * devices) == 0
+    fits = fits and (heads_width * args[4].shape[1]) % (devices * args[3].shape[1]) == 0
+    return local_by_head(*args) if fits else local(*args)
+
+
 def solution(mesh):
     return jax.shard_map(
-        local,
+        pick,
         mesh=mesh,
         in_specs=(
             P("dp", "seq", None),

time: 661 us -> 162 us (0.25)
  waiting for transfers between devices: 321 us -> 0 us
  matrix products: 126 us -> 19.6 us
  Pallas kernels: 0 us -> 102 us
  blocking collectives: 99.2 us -> 0 us
  starting transfers between devices: 24.8 us -> 0 us
  local copies, waits for them, and re-layouts: 37.8 us -> 17.7 us
  loops' own time: 15.8 us -> 0 us
  between operations: 14 us -> 2.73 us
    unnamed x17 -> x0, waiting for transfers between devices: 275 us -> none
    dot_general x56 -> x9, matrix products: 126 us -> 19.6 us  [the longest x1 5.29 us: local_by_head(): jnp.einsum('se,fe->sf', tile_grad.astype(BF16), proj_weight, preferred_el...]
    pallas_call x0 -> x3, Pallas kernels: none -> 102 us  [the longest x1 53.2 us: reduce_blocks(): pl.pallas_call(partial(reduce_kernel, bit_counts, orders), out_shape=[jax...]
    unnamed x1 -> x0, blocking collectives: 79.1 us -> none
    all_gather x1 -> x0, waiting for transfers between devices: 45.6 us -> none  [local(): lax.all_gather(saved[:, heads_width:], 'seq', axis=0, tiled=True)]
    unnamed x12 -> x0, starting transfers between devices: 24.7 us -> none
    unnamed x24 -> x18, local copies, waits for them, and re-layouts: 24 us -> 1.86 us
    all_to_all x1 -> x0, blocking collectives: 20.1 us -> none  [local(): lax.all_to_all(outgoing, 'seq', split_axis=0, concat_axis=0, tiled=True)]
  transfers between devices with their start and end apart: 13 -> 0, of which waited for: 5 -> 0; matrix products, arithmetic and copies ran while one was open for 19% -> 0% of each run, Pallas kernels for 0% -> 0%
where the time goes in v1:
time: 162 us
  Pallas kernels  102 us (63%)
  matrix products  19.6 us (12%)
  other arithmetic  19.5 us (12%)
  local copies, waits for them, and re-layouts  17.7 us (11%)
  between operations  2.73 us (2%)
    pallas_call x1, Pallas kernels, reduce_blocks(): pl.pallas_call(partial(reduce_kernel, bit_counts, orders), out_shape=[jax...  53.2 us
    pallas_call x1, Pallas kernels, attention_by_head(): pl.pallas_call(partial(attention_kernel, count, width, scaling), out_shap...  33.8 us
    pallas_call x1, Pallas kernels, exchange(): pl.pallas_call(partial(exchange_kernel, count), out_shape=jax.ShapeDtypeS...  14.9 us
    add x2, other arithmetic, local_by_head(): ids = pos // span * stride + pos % stride  14.5 us
    dot_general x1, matrix products, local_by_head(): jnp.einsum('se,fe->sf', tile_grad.astype(BF16), proj_weight, preferred_el...  5.29 us
    convert_element_type x1, local copies, waits for them, and re-layouts, local_by_head(): embed_term.astype(BF16).reshape(tile_shape)  4.38 us
    convert_element_type x1, local copies, waits for them, and re-layouts, local_by_head(): factor_term.astype(BF16).reshape(tile_shape)  4.27 us
    dot_general x1, matrix products, local_by_head(): jnp.einsum('sc,sd->cd', tile_output[0], incoming, preferred_element_type=...  3.5 us

profile of v1, /device:TPU:0, one launch (start us, length us, event | category | flops | bytes accessed | tf_op | source)
XLA Modules:
  0.0 161.5 jit_solution(633882506742109729)
XLA Ops:
  0.6 0.0 copy-start
  0.7 1.4 dynamic_slice.8
  3.3 1.2 dynamic_slice.7
  5.2 12.0 %fusion.8.id_column = s32[1024,1]{1,0:T(8,128)} fusion(s32[]{:T(128)S(6)} %select_n.53, s32[]{:T(128)} %bitcast.8, s32[]{:T(128)} %bitcast.7, s32[]{:T(128)S(6)} %sign.25, pred[]{:T(512)S(6)} %lt.31), kind=kLoop, calls=%fused_computation.21 | loop fusion | flops 17408 | bytes 4113 | tf_op jit(solution)/shard_map/add | solution.py:482
  17.2 2.5 %fusion.24.id_row = s32[8,1,128]{2,1,0:T(1,128)} fusion(pred[]{:T(512)S(6)} %lt.31, s32[]{:T(128)S(6)} %select_n.53, s32[]{:T(128)} %bitcast.8, s32[]{:T(128)} %bitcast.7, s32[]{:T(128)S(6)} %sign.25), kind=kLoop, calls=%fused_computation.48 | loop fusion | flops 19456 | bytes 4113 | tf_op jit(solution)/shard_map/add | solution.py:482
  19.8 1.2 copy.26
  20.9 1.5 convolution_convert_fusion.7
  22.4 0.8 copy.27
  23.2 33.8 %head_attention.1 = bf16[8,192,128]{2,1,0:T(8,128)(2,1)} custom-call(bf16[8,192,128]{2,1,0:T(8,128)(2,1)} %bitcast.70, s32[1024,1]{1,0:T(8,128)} %fusion.8.id_column, s32[8,1,128]{2,1,0:T(1,128)} %fusion.24.id_row), custom_call_target="tpu_custom_call" | custom-call | tf_op jit(solution)/shard_map/head_attention/pallas_call | solution.py:293
  57.0 1.0 copy.32
  58.1 0.0 copy-done.4
  58.1 1.9 %convolution_convert_fusion.2 = bf16[1152,768]{0,1:T(8,128)(2,1)} fusion(bf16[1152,128]{1,0:T(8,128)(2,1)S(1)} %bitcast.65, bf16[1,128,768]{2,1,0:T(8,128)(2,1)S(1)} %copy-done.4), kind=kOutput, calls=%fused_computation.2 | convolution fusion | flops 227377152 | bytes 2260992 | tf_op jit(solution)/shard_map/tc,kt->ck/dot_general | solution.py:495
  60.0 1.1 convolution_convert_fusion.5
  61.1 1.5 concatenate.16
  62.6 0.0 copy-start.7
  62.6 3.2 %pad_maximum_fusion.refs_0_ = bf16[2,2,2,2,2,32,1152]{6,5,4,3,2,1,0:T(8,128)(2,1)} fusion(bf16[2,2,2,2,2,8,1152]{6,5,4,3,2,1,0:T(8,128)(2,1)S(1)} %concatenate.16, bf16[2,2,2,2,2,24,1152]{6,5,4,3,2,1,0:T(8,128)(2,1)} %bitcast.61), kind=kLoop, calls=%fused_computation.8 | loop fusion | flops 4718592 | bytes 4718592 | tf_op jit(solution)/shard_map/concatenate | solution.py:501
  65.8 0.0 copy-done.7
  65.8 0.1 fusion.4
  65.9 3.1 %convolution_convert_fusion.6 = bf16[256,768]{1,0:T(8,128)(2,1)} fusion(bf16[1152,128]{1,0:T(8,128)(2,1)S(1)} %bitcast.66, bf16[768,1152]{1,0:T(8,128)(2,1)} %param.15, bf16[1,128,768]{2,1,0:T(8,128)(2,1)S(1)} %copy-done.2, s32[128]{0:T(128)S(1)} %convert_add_fusion), kind=kOutput, calls=%fused_computation.10 | convolution fusion | flops 277348352 | bytes 2654720 | tf_op jit(solution)/shard_map/dot_general | solution.py:446
  69.1 14.9 %tile_exchange.1 = bf16[8,32,768]{2,1,0:T(8,128)(2,1)} custom-call(bf16[8,32,768]{2,1,0:T(8,128)(2,1)} %bitcast.72), custom_call_target="tpu_custom_call" | custom-call | tf_op jit(solution)/shard_map/tile_exchange/pallas_call | solution.py:195
  84.0 3.5 %fusion = bf16[1536,768]{0,1:T(8,128)(2,1)} fusion(bf16[256,768]{1,0:T(8,128)(2,1)} %bitcast.62, bf16[1,256,1536]{2,1,0:T(8,128)(2,1)} %param.21), kind=kOutput, calls=%fused_computation.3 | convolution fusion | flops 605159424 | bytes 3538944 | tf_op jit(solution)/shard_map/sc,sd->cd/dot_general | solution.py:508
  87.5 4.4 %copy.29 = bf16[1536,768]{1,0:T(8,128)(2,1)} copy(bf16[1536,768]{0,1:T(8,128)(2,1)} %fusion) | data formatting | bytes 4718592 | tf_op jit(solution)/shard_map/convert_element_type | solution.py:528
  91.9 2.3 %fusion.1 = bf16[1536,768]{0,1:T(8,128)(2,1)} fusion(bf16[256,768]{1,0:T(8,128)(2,1)S(1)} %bitcast.63, bf16[1,256,1536]{2,1,0:T(8,128)(2,1)S(1)} %copy-done.3), kind=kOutput, calls=%fused_computation.4 | convolution fusion | flops 605159424 | bytes 3538944 | tf_op jit(solution)/shard_map/sc,sd->cd/dot_general | solution.py:509
  94.1 4.3 %copy.30 = bf16[1536,768]{1,0:T(8,128)(2,1)} copy(bf16[1536,768]{0,1:T(8,128)(2,1)} %fusion.1) | data formatting | bytes 4718592 | tf_op jit(solution)/shard_map/convert_element_type | solution.py:529
  98.4 53.2 %reduce_blocks.1 = (f32[32,1152]{1,0:T(8,128)}, f32[48,768]{1,0:T(8,128)}, f32[48,768]{1,0:T(8,128)}) custom-call(bf16[2,2,2,2,2,32,1152]{6,5,4,3,2,1,0:T(8,128)(2,1)} %pad_maximum_fusion.refs_0_, bf16[2,2,2,2,2,48,768]{6,5,4,3,2,1,0:T(8,128)(2,1)} %bitcast.59, bf16[2,2,2,2,2,48,768]{6,5,4,3,2,1,0:T(8,128)(2,1)} %bitcast.60), custom_call_target="tpu_custom_call" | custom-call | tf_op jit(solution)/shard_map/reduce_blocks/pallas_call | solution.py:415
  151.6 1.0 subtract_convert_fusion
  152.7 0.8 fusion.19
  153.5 0.8 slice_add_fusion
  154.3 0.7 slice.22
  154.9 0.6 reshape.186
  155.6 5.3 %fusion.2 = bf16[1,256,1536]{2,1,0:T(8,128)(2,1)} fusion(bf16[1536,1536]{1,0:T(8,128)(2,1)} %param.23, bf16[256,768]{1,0:T(8,128)(2,1)S(1)} %bitcast.64, bf16[1536,768]{1,0:T(8,128)(2,1)S(1)} %copy-done), kind=kOutput, calls=%fused_computation.7 | convolution fusion | flops 1812725760 | bytes 8257536 | tf_op jit(solution)/shard_map/se,fe->sf/dot_general | solution.py:513
  160.8 0.7 copy.34
  (17 shorter events, 0.1 us)
Async XLA Ops:
  0.6 152.0 %copy-start = (bf16[1536,768]{1,0:T(8,128)(2,1)S(1)}, bf16[1536,768]{1,0:T(8,128)(2,1)}, u32[]{:S(2)}) copy-start(bf16[1536,768]{1,0:T(8,128)(2,1)} %param.22) | copy-start | bytes 7077892
  20.9 37.2 %copy-start.4 = (bf16[1,128,768]{2,1,0:T(8,128)(2,1)S(1)}, bf16[1,128,768]{2,1,0:T(8,128)(2,1)}, u32[]{:S(2)}) copy-start(bf16[1,128,768]{2,1,0:T(8,128)(2,1)} %param.12) | copy-start | bytes 589828
  23.2 36.8 %copy-start.2 = (bf16[1,128,768]{2,1,0:T(8,128)(2,1)S(1)}, bf16[1,128,768]{2,1,0:T(8,128)(2,1)}, u32[]{:S(2)}) copy-start(bf16[1,128,768]{2,1,0:T(8,128)(2,1)} %param.14) | copy-start | bytes 589828
  62.6 3.2 %copy-start.7 = (s32[1,128,1]{1,2,0:T(1,128)S(1)}, s32[1,128,1]{1,2,0:T(1,128)}, u32[]{:S(2)}) copy-start(s32[1,128,1]{1,2,0:T(1,128)} %param.19) | copy-start | bytes 1540
  87.5 4.4 %copy-start.1 = (bf16[8,32,768]{2,1,0:T(8,128)(2,1)S(1)}, bf16[8,32,768]{2,1,0:T(8,128)(2,1)}, u32[]{:S(2)}) copy-start(bf16[8,32,768]{2,1,0:T(8,128)(2,1)} %tile_exchange.1) | copy-start | bytes 1179652
  87.5 4.4 %copy-start.3 = (bf16[1,256,1536]{2,1,0:T(8,128)(2,1)S(1)}, bf16[1,256,1536]{2,1,0:T(8,128)(2,1)}, u32[]{:S(2)}) copy-start(bf16[1,256,1536]{2,1,0:T(8,128)(2,1)} %param.20) | copy-start | bytes 2359300
  151.6 2.7 %copy-start.5 = (f32[32,1152]{1,0:T(8,128)S(1)}, f32[32,1152]{1,0:T(8,128)}, u32[]{:S(2)}) copy-start(f32[32,1152]{1,0:T(8,128)} %get-tuple-element.10) | copy-start | bytes 442372
  155.6 5.3 %copy-start.6 = (f32[48,768]{1,0:T(8,128)S(1)}, f32[48,768]{1,0:T(8,128)}, u32[]{:S(2)}) copy-start(f32[48,768]{1,0:T(8,128)} %get-tuple-element.20) | copy-start | bytes 442372
